TPU v7x, 32 devices: a whole 2x2x4 slice. The times are simulated.
32 devices in a mesh: grp: 2 (over y), rows: 8 (over z, x), mod: 2 (over core).
Axes of the slice: x: 2, y: 2, z: 4, core: 2. Of those that a mesh axis runs over, the one named last changes fastest.
Arguments:
- queries: bfloat16 [16, 8, 2304], P(('grp', 'rows'), 'mod'), parts along dimension 0, may hold values from -6 to 6
- train_grads: bfloat16 [2048, 8, 2304], P(('grp', 'rows'), 'mod'), parts along dimension 0, may hold values from -6 to 6
- factors: float32 [8, 2, 48, 48], P('mod'), may hold values from -4 to 4, as said below
Outputs:
- scores: float32 [16, 1024], P(('grp', 'mod'), 'rows'), parts along dimension 0
There are 2 independent parts, one for each index of `grp`. A program takes and returns all parts, laid end to end along the dimension named above; an argument that names none is the same for every part. Nothing has to cross between parts.
Inputs may be any that keep to these rules, and one draw needn't show every extreme that they name: `factors`: each factor is a 48 x 48 matrix with a positive diagonal and full rank.
All inputs are finite; a program needn't handle non-finite values.
Results may differ from a plain program's by a relative error of at most 0.0029.
Values may be sent and summed in bfloat16 or wider, within the bound.
No kernel may reach another device: no remote copies, remote signals or barrier semaphores. Data moves between devices by JAX's collectives and lax.ppermute only.
A program may use at most 64 MiB of HBM per device.

v0:
```python
import functools
import math

import jax
import jax.numpy as jnp
import numpy as np
from jax import lax
from jax.experimental import pallas as pl
from jax.experimental.pallas import tpu as pltpu
from jax.sharding import PartitionSpec as P


DIRECT_PLANES = 4

HI = lax.Precision.HIGHEST
NT = (((1,), (1,)), ((), ()))
NN = (((1,), (0,)), ((), ()))


def lane_masks(proj):
    width = math.lcm(proj, 128)
    held = width // proj
    lane = lax.broadcasted_iota(jnp.int32, (held, width), 1)
    first = lax.broadcasted_iota(jnp.int32, (held, width), 0) * proj
    mine = jnp.logical_and(lane >= first, lane < first + proj)
    column = lax.broadcasted_iota(jnp.int32, (proj, width), 1)
    column = column - column // proj * proj
    pick = (column == lax.broadcasted_iota(jnp.int32, (proj, width), 0)).astype(jnp.bfloat16)
    return mine, pick


def squares(query, mine, pick):
    query = query.astype(jnp.float32)
    held, width = mine.shape
    spread = []
    for m in range(query.shape[0]):
        for at in range(0, query.shape[1], width):
            part = jnp.broadcast_to(query[m : m + 1, at : at + width], (held, width))
            spread.append(jnp.where(mine, part, 0.0))
    spread = jnp.concatenate(spread, axis=0).astype(jnp.bfloat16)
    return lax.dot_general(spread, pick, NT, preferred_element_type=jnp.float32)


def both_sides(square, f_ref, scale):
    proj = f_ref.shape[-1]
    both = []
    rights = [lax.dot_general(
        square[m * proj : (m + 1) * proj], f_ref[m, 1], NN,
        precision=HI, preferred_element_type=jnp.float32) for m in range(f_ref.shape[0])]
    for m in range(f_ref.shape[0]):
        both.append(lax.dot_general(
            f_ref[m, 0], rights[m], NN, precision=HI, preferred_element_type=jnp.float32))
    return (jnp.concatenate(both, axis=0) / scale).astype(jnp.bfloat16)


def flatten(both, mine, pick, rows_ref):
    held, width = mine.shape
    wide = lax.dot_general(both, pick, NN, preferred_element_type=jnp.float32)
    at = 0
    for m in range(rows_ref.shape[0]):
        for lanes in range(0, rows_ref.shape[1], width):
            rows_ref[m : m + 1, lanes : lanes + width] = jnp.sum(
                jnp.where(mine, wide[at : at + held], 0.0), axis=0, keepdims=True)
            at += held


def first_kernel(scale, q_hbm, f_hbm, o_ref, f_ref, q_ref, rows_ref, sems):
    copies = [pltpu.make_async_copy(q_hbm, q_ref, sems.at[0])]
    copies += [pltpu.make_async_copy(f_hbm.at[:, j], f_ref.at[:, j], sems.at[2 - j]) for j in (1, 0)]
    for copy in copies:
        copy.start()
    mine, pick = lane_masks(f_ref.shape[-1])
    copies[0].wait()
    for i in range(q_ref.shape[0]):
        square = squares(q_ref[i], mine, pick)
        if i == 0:
            copies[1].wait()
            copies[2].wait()
        flatten(both_sides(square, f_ref, scale), mine, pick, rows_ref)
        o_ref[i] = rows_ref[...].astype(jnp.bfloat16)


def second_kernel(scale, own_ref, q_ref, f_ref, o_ref, rows_ref):
    count = own_ref.shape[0]
    mine, pick = lane_masks(f_ref.shape[-1])
    o_ref[:count] = own_ref[...]
    for i in range(count):
        flatten(both_sides(squares(q_ref[i], mine, pick), f_ref, scale), mine, pick, rows_ref)
        o_ref[count + i] = rows_ref[...].astype(jnp.bfloat16)


def precondition(queries, factors, modules):
    scale = float(np.sqrt(np.float32(modules * queries.shape[2])))
    hbm, vmem = pl.BlockSpec(memory_space=pltpu.HBM), pl.BlockSpec(memory_space=pltpu.VMEM)
    return pl.pallas_call(
        functools.partial(first_kernel, scale),
        out_shape=(pltpu.VMEM(queries.shape, jnp.bfloat16), pltpu.VMEM(factors.shape, factors.dtype)),
        in_specs=[hbm, hbm],
        out_specs=(vmem, vmem),
        scratch_shapes=[
            pltpu.VMEM(queries.shape, queries.dtype),
            pltpu.VMEM(queries.shape[1:], jnp.float32),
            pltpu.SemaphoreType.DMA((3,)),
        ],
        compiler_params=pltpu.CompilerParams(vmem_limit_bytes=8 << 20),
        cost_estimate=pl.CostEstimate(
            flops=24 * queries.size * factors.shape[-1], bytes_accessed=4 * (queries.size + factors.size),
            transcendentals=0),
        name="precondition_own",
    )(*(pltpu.with_memory_space_constraint(a, pltpu.HBM) for a in (queries, factors)))


def precondition_more(own, queries, factors, modules):
    scale = float(np.sqrt(np.float32(modules * queries.shape[2])))
    vmem = pl.BlockSpec(memory_space=pltpu.VMEM)
    return pl.pallas_call(
        functools.partial(second_kernel, scale),
        out_shape=pltpu.VMEM((2 * own.shape[0], *own.shape[1:]), own.dtype),
        in_specs=[vmem] * 3,
        out_specs=vmem,
        scratch_shapes=[pltpu.VMEM(queries.shape[1:], jnp.float32)],
        compiler_params=pltpu.CompilerParams(vmem_limit_bytes=8 << 20),
        name="precondition_neighbour",
    )(own, queries, factors)


def dot_rows(ready, train_grads):
    return lax.dot_general(
        ready, train_grads, (((1, 2), (1, 2)), ((), ())), preferred_element_type=jnp.float32
    )


def send_rows(x, target):
    return lax.ppermute(x, "rows", [(r, target(r)) for r in range(lax.axis_size("rows"))])


def named(x, axes, target):
    return lax.ppermute(x, axes, [(i, target(i)) for i in range(lax.axis_size(axes))])


def scores_direct(queries, train_grads, factors, modules, rows):
    planes = rows // 2
    plane, odd, low = lax.axis_index("rows") // 2, lax.axis_index("rows") % 2, lax.axis_index("mod") == 0
    neighbour = send_rows(queries, lambda r: r ^ 1)
    own, tables = precondition(queries, factors, modules)
    pair = precondition_more(own, neighbour, tables, modules)
    far = [named(pair, ("rows", "mod"), lambda i: ((i // 2 + 2) % rows) * 2 + 1 - i % 2)]
    for s in range(2, planes):
        far.append(named(pair, "rows", lambda r, s=s: (r + 2 * s) % rows))
    far[0] = named(far[0], "mod", lambda c: 1 - c)
    count = queries.shape[0]

    def products(pieces):
        part = dot_rows(jnp.concatenate(pieces), train_grads).reshape(len(pieces), 2, count, -1)
        return jnp.where(odd == 0, part, part[:, ::-1])

    early = products([pair] + far[1:-1])
    early = jnp.concatenate([early[:1], jnp.zeros_like(early[:1]), early[1:], jnp.zeros_like(early[:1])])
    early = jnp.stack([early[-p % planes] for p in range(planes)])
    step = 1
    while step < planes:
        early = jnp.where(plane & step == 0, early, jnp.roll(early, step, axis=0))
        step *= 2
    half = planes // 2
    late = products([far[0], far[-1]])
    place = jnp.arange(half)[:, None, None, None]

    def whole(kept, first):
        where = place + first
        kept = jnp.where(where == (plane - 1) % planes, late[:1], kept)
        kept = jnp.where(where == (plane + 1) % planes, late[1:], kept)
        return kept.reshape(rows // 2 * count, -1)

    keep = whole(jnp.where(low, early[:half], early[half:]), jnp.where(low, 0, half))
    give = whole(jnp.where(low, early[half:], early[:half]), jnp.where(low, half, 0))
    return keep + lax.ppermute(give, "mod", [(0, 1), (1, 0)])


def scores_gathered(own, train_grads):
    part = dot_rows(lax.all_gather(own, "rows", axis=0, tiled=True), train_grads)
    return lax.psum_scatter(part, "mod", scatter_dimension=0, tiled=True)


def goes_direct(rows, cores):
    return cores == 2 and rows == 2 * DIRECT_PLANES


def shards(queries, train_grads, factors):
    modules = queries.shape[1] * lax.axis_size("mod")
    rows = lax.axis_size("rows")
    if goes_direct(rows, lax.axis_size("mod")):
        return scores_direct(queries, train_grads, factors, modules, rows)
    return scores_gathered(precondition(queries, factors, modules)[0], train_grads)


def solution(mesh):
    in_specs = (
        P(("grp", "rows"), "mod", None),
        P(("grp", "rows"), "mod", None),
        P("mod", None, None, None),
    )
    out_specs = P(("grp", "mod"), "rows")
    return jax.shard_map(shards, mesh=mesh, in_specs=in_specs, out_specs=out_specs, check_vma=False)
```

profile of v0, /device:TPU:0, one launch (start us, length us, event | category | flops | bytes accessed | tf_op | source)
XLA Modules:
  0.0 15.8 jit_solution(14788163424771545752)
XLA Ops:
  0.0 0.0 copy-start
  0.0 3.0 %collective-permute-start = (bf16[1,4,2304]{2,1,0:T(4,128)(2,1)}, bf16[1,4,2304]{2,1,0:T(4,128)(2,1)S(1)}, u32[]{:S(2)}, u32[]{:S(2)}) collective-permute-start(bf16[1,4,2304]{2,1,0:T(4,128)(2,1)} %q_hbm.1), channel_id=1, source_target_pairs={{0,2},{2,0},{4,6},{6,4},{8,10},{10,8},{12,14},{14,12},{1,3},{3,1},... | collective-permute-start | bytes 55304 | tf_op jit(solution)/shard_map/ppermute | solution.py:134
  3.0 1.6 %precondition_own.1 = (bf16[1,4,2304]{2,1,0:T(4,128)(2,1)S(1)}, f32[4,2,48,48]{3,2,1,0:T(8,128)S(1)}) custom-call(bf16[1,4,2304]{2,1,0:T(4,128)(2,1)} %q_hbm.1, f32[4,2,48,48]{3,2,1,0:T(8,128)} %f_hbm.1), custom_call_target="tpu_custom_call" | custom-call | flops 10616832 | bytes 110592 | tf_op jit(solution)/shard_map/precondition_own/pallas_call | solution.py:95
  4.5 0.4 %collective-permute-done.q_ref = bf16[1,4,2304]{2,1,0:T(4,128)(2,1)S(1)} collective-permute-done((bf16[1,4,2304]{2,1,0:T(4,128)(2,1)}, bf16[1,4,2304]{2,1,0:T(4,128)(2,1)S(1)}, u32[]{:S(2)}, u32[]{:S(2)}) %collective-permute-start) | collective-permute-done | bytes 18464 | tf_op jit(solution)/shard_map/ppermute | solution.py:134
  4.9 0.7 %precondition_neighbour.1 = bf16[2,4,2304]{2,1,0:T(4,128)(2,1)S(1)} custom-call(bf16[1,4,2304]{2,1,0:T(4,128)(2,1)S(1)} %get-tuple-element.7.own_ref, bf16[1,4,2304]{2,1,0:T(4,128)(2,1)S(1)} %collective-permute-done.q_ref, f32[4,2,48,48]{3,2,1,0:T(8,128)S(1)} %get-tuple-element.8.f_ref), custom_call_target="tpu_custom_call" | custom-call | tf_op jit(solution)/shard_map/precondition_neighbour/pallas_call | solution.py:116
  5.6 0.5 %collective-permute-start.1 = (bf16[2,4,2304]{2,1,0:T(4,128)(2,1)S(1)}, bf16[2,4,2304]{2,1,0:T(4,128)(2,1)S(1)}, u32[]{:S(2)}, u32[]{:S(2)}) collective-permute-start(bf16[2,4,2304]{2,1,0:T(4,128)(2,1)S(1)} %precondition_neighbour.1), channel_id=1, source_target_pairs={{0,5},{1,4},{2,7},{3,6},{4,9},{5,8},{6,11},{7,10},{8,13},{9,12},{1... | collective-permute-start | bytes 110600 | tf_op jit(solution)/shard_map/ppermute | solution.py:138
  6.1 2.8 %collective-permute-start.4 = (bf16[2,4,2304]{2,1,0:T(4,128)(2,1)S(1)}, bf16[2,4,2304]{2,1,0:T(4,128)(2,1)S(1)}, u32[]{:S(2)}, u32[]{:S(2)}) collective-permute-start(bf16[2,4,2304]{2,1,0:T(4,128)(2,1)S(1)} %precondition_neighbour.1), channel_id=1, source_target_pairs={{0,8},{2,10},{4,12},{6,14},{8,0},{10,2},{12,4},{14,6},{1,9},{3,11}... | collective-permute-start | bytes 110600 | tf_op jit(solution)/shard_map/ppermute | solution.py:138
  8.9 1.3 %collective-permute-start.3 = (bf16[2,4,2304]{2,1,0:T(4,128)(2,1)S(1)}, bf16[2,4,2304]{2,1,0:T(4,128)(2,1)S(1)}, u32[]{:S(2)}, u32[]{:S(2)}) collective-permute-start(bf16[2,4,2304]{2,1,0:T(4,128)(2,1)S(1)} %precondition_neighbour.1), channel_id=1, source_target_pairs={{0,12},{2,14},{4,0},{6,2},{8,4},{10,6},{12,8},{14,10},{1,13},{3,15... | collective-permute-start | bytes 110600 | tf_op jit(solution)/shard_map/ppermute | solution.py:138
  10.2 0.7 %collective-permute-done.1 = bf16[2,4,2304]{2,1,0:T(4,128)(2,1)S(1)} collective-permute-done((bf16[2,4,2304]{2,1,0:T(4,128)(2,1)S(1)}, bf16[2,4,2304]{2,1,0:T(4,128)(2,1)S(1)}, u32[]{:S(2)}, u32[]{:S(2)}) %collective-permute-start.1) | collective-permute-done | bytes 36896 | tf_op jit(solution)/shard_map/ppermute | solution.py:138
  10.9 0.7 %collective-permute-start.2 = (bf16[2,4,2304]{2,1,0:T(4,128)(2,1)S(1)}, bf16[2,4,2304]{2,1,0:T(4,128)(2,1)S(1)}, u32[]{:S(2)}, u32[]{:S(2)}) collective-permute-start(bf16[2,4,2304]{2,1,0:T(4,128)(2,1)S(1)} %collective-permute-done.1), channel_id=1, source_target_pairs={{0,1},{1,0},{2,3},{3,2},{4,5},{5,4},{6,7},{7,6},{8,9},{9,8},{10,11... | collective-permute-start | bytes 110600 | tf_op jit(solution)/shard_map/ppermute | solution.py:138
  11.6 0.0 collective-permute-done.4
  11.6 0.1 pad_maximum_fusion.1
  11.7 0.0 copy-done
  11.7 0.7 %fusion = f32[4,128,1]{1,0,2:T(4,128)S(1)} fusion(bf16[128,4,2304]{2,1,0:T(4,128)(2,1)S(1)} %copy-done, bf16[4,4,2304]{2,1,0:T(4,128)(2,1)S(1)} %pad_maximum_fusion.1), kind=kOutput, calls=%fused_computation | convolution fusion | flops 9437184 | bytes 2435072 | tf_op jit(solution)/shard_map/dot_general | solution.py:128
  12.4 0.7 %collective-permute-done.3 = bf16[2,4,2304]{2,1,0:T(4,128)(2,1)S(1)} collective-permute-done((bf16[2,4,2304]{2,1,0:T(4,128)(2,1)S(1)}, bf16[2,4,2304]{2,1,0:T(4,128)(2,1)S(1)}, u32[]{:S(2)}, u32[]{:S(2)}) %collective-permute-start.3) | collective-permute-done | bytes 36896 | tf_op jit(solution)/shard_map/ppermute | solution.py:138
  13.1 0.0 collective-permute-done.2
  13.1 0.1 pad_maximum_fusion
  13.2 0.7 %fusion.2 = f32[4,128,1]{1,0,2:T(4,128)S(1)} fusion(bf16[128,4,2304]{2,1,0:T(4,128)(2,1)S(1)} %copy-done, bf16[4,4,2304]{2,1,0:T(4,128)(2,1)S(1)} %pad_maximum_fusion), kind=kOutput, calls=%fused_computation.2 | convolution fusion | flops 9437184 | bytes 2435072 | tf_op jit(solution)/shard_map/dot_general | solution.py:128
  14.0 0.1 select_select_fusion
  14.1 0.2 %collective-permute-start.5 = (f32[4,128]{1,0:T(4,128)S(1)}, f32[4,128]{1,0:T(4,128)S(1)}, u32[]{:S(2)}, u32[]{:S(2)}) collective-permute-start(f32[4,128]{1,0:T(4,128)S(1)} %bitcast.17), channel_id=1, source_target_pairs={{0,1},{1,0},{2,3},{3,2},{4,5},{5,4},{6,7},{7,6},{8,9},{9,8},{10,11... | collective-permute-start | bytes 6152 | tf_op jit(solution)/shard_map/ppermute | solution.py:176
  14.3 0.9 %collective-permute-done.5 = f32[4,128]{1,0:T(4,128)S(1)} collective-permute-done((f32[4,128]{1,0:T(4,128)S(1)}, f32[4,128]{1,0:T(4,128)S(1)}, u32[]{:S(2)}, u32[]{:S(2)}) %collective-permute-start.5) | collective-permute-done | bytes 2080 | tf_op jit(solution)/shard_map/ppermute | solution.py:176
  15.2 0.6 %add.59 = f32[4,128]{1,0:T(4,128)} add(f32[4,128]{1,0:T(4,128)S(1)} %bitcast.12, f32[4,128]{1,0:T(4,128)S(1)} %collective-permute-done.5) | non-fusion elementwise | flops 512 | bytes 6144 | tf_op jit(solution)/shard_map/add | solution.py:176
  (11 shorter events, 0.1 us)
Async XLA Ops:
  0.0 11.7 %copy-start = (bf16[128,4,2304]{2,1,0:T(4,128)(2,1)S(1)}, bf16[128,4,2304]{2,1,0:T(4,128)(2,1)}, u32[]{:S(2)}) copy-start(bf16[128,4,2304]{2,1,0:T(4,128)(2,1)} %param.4) | copy-start | bytes 7077892
  0.0 4.9 %collective-permute-start = (bf16[1,4,2304]{2,1,0:T(4,128)(2,1)}, bf16[1,4,2304]{2,1,0:T(4,128)(2,1)S(1)}, u32[]{:S(2)}, u32[]{:S(2)}) collective-permute-start(bf16[1,4,2304]{2,1,0:T(4,128)(2,1)} %q_hbm.1), channel_id=1, source_target_pairs={{0,2},{2,0},{4,6},{6,4},{8,10},{10,8},{12,14},{14,12},{1,3},{3,1},... | collective-permute-start | bytes 55304 | tf_op jit(solution)/shard_map/ppermute | solution.py:134
  5.6 5.3 %collective-permute-start.1 = (bf16[2,4,2304]{2,1,0:T(4,128)(2,1)S(1)}, bf16[2,4,2304]{2,1,0:T(4,128)(2,1)S(1)}, u32[]{:S(2)}, u32[]{:S(2)}) collective-permute-start(bf16[2,4,2304]{2,1,0:T(4,128)(2,1)S(1)} %precondition_neighbour.1), channel_id=1, source_target_pairs={{0,5},{1,4},{2,7},{3,6},{4,9},{5,8},{6,11},{7,10},{8,13},{9,12},{1... | collective-permute-start | bytes 110600 | tf_op jit(solution)/shard_map/ppermute | solution.py:138
  6.1 5.5 %collective-permute-start.4 = (bf16[2,4,2304]{2,1,0:T(4,128)(2,1)S(1)}, bf16[2,4,2304]{2,1,0:T(4,128)(2,1)S(1)}, u32[]{:S(2)}, u32[]{:S(2)}) collective-permute-start(bf16[2,4,2304]{2,1,0:T(4,128)(2,1)S(1)} %precondition_neighbour.1), channel_id=1, source_target_pairs={{0,8},{2,10},{4,12},{6,14},{8,0},{10,2},{12,4},{14,6},{1,9},{3,11}... | collective-permute-start | bytes 110600 | tf_op jit(solution)/shard_map/ppermute | solution.py:138
  8.9 4.2 %collective-permute-start.3 = (bf16[2,4,2304]{2,1,0:T(4,128)(2,1)S(1)}, bf16[2,4,2304]{2,1,0:T(4,128)(2,1)S(1)}, u32[]{:S(2)}, u32[]{:S(2)}) collective-permute-start(bf16[2,4,2304]{2,1,0:T(4,128)(2,1)S(1)} %precondition_neighbour.1), channel_id=1, source_target_pairs={{0,12},{2,14},{4,0},{6,2},{8,4},{10,6},{12,8},{14,10},{1,13},{3,15... | collective-permute-start | bytes 110600 | tf_op jit(solution)/shard_map/ppermute | solution.py:138
  10.9 2.2 %collective-permute-start.2 = (bf16[2,4,2304]{2,1,0:T(4,128)(2,1)S(1)}, bf16[2,4,2304]{2,1,0:T(4,128)(2,1)S(1)}, u32[]{:S(2)}, u32[]{:S(2)}) collective-permute-start(bf16[2,4,2304]{2,1,0:T(4,128)(2,1)S(1)} %collective-permute-done.1), channel_id=1, source_target_pairs={{0,1},{1,0},{2,3},{3,2},{4,5},{5,4},{6,7},{7,6},{8,9},{9,8},{10,11... | collective-permute-start | bytes 110600 | tf_op jit(solution)/shard_map/ppermute | solution.py:138
  14.1 1.2 %collective-permute-start.5 = (f32[4,128]{1,0:T(4,128)S(1)}, f32[4,128]{1,0:T(4,128)S(1)}, u32[]{:S(2)}, u32[]{:S(2)}) collective-permute-start(f32[4,128]{1,0:T(4,128)S(1)} %bitcast.17), channel_id=1, source_target_pairs={{0,1},{1,0},{2,3},{3,2},{4,5},{5,4},{6,7},{7,6},{8,9},{9,8},{10,11... | collective-permute-start | bytes 6152 | tf_op jit(solution)/shard_map/ppermute | solution.py:176
where the time goes:
time: 16 us; the launch traced here: 15.8 us
  starting transfers between devices  8.49 us (53%)
  waiting for transfers between devices  2.67 us (17%)
  Pallas kernels  2.28 us (14%)
  matrix products  1.41 us (9%)
  other arithmetic  0.8 us (5%)
    ppermute x4, starting transfers between devices, named(): lax.ppermute(x, axes, [(i, target(i)) for i in range(lax.axis_size(axes))])  5.29 us
    ppermute x1, starting transfers between devices, send_rows(): lax.ppermute(x, 'rows', [(r, target(r)) for r in range(lax.axis_size('row...  2.97 us
    pallas_call x1, Pallas kernels, precondition(): pl.pallas_call(functools.partial(first_kernel, scale), out_shape=(pltpu.V...  1.56 us
    dot_general x2, matrix products, dot_rows(): lax.dot_general(ready, train_grads, (((1, 2), (1, 2)), ((), ())), preferr...  1.41 us
    ppermute x4, waiting for transfers between devices, named(): lax.ppermute(x, axes, [(i, target(i)) for i in range(lax.axis_size(axes))])  1.35 us
    ppermute x1, waiting for transfers between devices, scores_direct(): return keep + lax.ppermute(give, 'mod', [(0, 1), (1, 0)])  0.95 us
    pallas_call x1, Pallas kernels, precondition_more(): pl.pallas_call(functools.partial(second_kernel, scale), out_shape=pltpu.V...  0.72 us
    add x1, other arithmetic, scores_direct(): return keep + lax.ppermute(give, 'mod', [(0, 1), (1, 0)])  0.58 us
  transfers between devices with their start and end apart: 6, of which 4 were waited for; matrix products, arithmetic and copies ran while one was open for 5% of the time, Pallas kernels for 10%

commit v1 on v0

--- a/solution.py
+++ b/solution.py
@@ -53,15 +53,38 @@
     return (jnp.concatenate(both, axis=0) / scale).astype(jnp.bfloat16)
 
 
+def column_sums(parts):
+    row = lax.broadcasted_iota(jnp.int32, parts[0].shape, 0)
+    rows = step = len(parts)
+    while step > 1:
+        step //= 2
+        upper = row & step == 0
+        joined = []
+        for a, b in zip(parts[:step], parts[step:]):
+            if 2 * step == rows:
+                joined.append(jnp.where(upper, a, b) + pltpu.roll(jnp.where(upper, b, a), step, 0))
+            else:
+                a, b = a + pltpu.roll(a, rows - step, 0), b + pltpu.roll(b, step, 0)
+                joined.append(jnp.where(upper, a, b))
+        parts = joined
+    return parts[0]
+
+
 def flatten(both, mine, pick, rows_ref):
     held, width = mine.shape
+    modules, coords = rows_ref.shape
+    groups = coords // width
     wide = lax.dot_general(both, pick, NN, preferred_element_type=jnp.float32)
-    at = 0
-    for m in range(rows_ref.shape[0]):
-        for lanes in range(0, rows_ref.shape[1], width):
-            rows_ref[m : m + 1, lanes : lanes + width] = jnp.sum(
-                jnp.where(mine, wide[at : at + held], 0.0), axis=0, keepdims=True)
-            at += held
+    parts = [
+        [jnp.where(mine, wide[at : at + held], 0.0) for at in range(m * groups * held, (m + 1) * groups * held, held)]
+        for m in range(modules)
+    ]
+    at = held // modules
+    for g in range(0, groups, at):
+        sums = column_sums([parts[m][g + i] for i in range(at) for m in range(modules)])
+        for i in range(at):
+            lanes = slice((g + i) * width, (g + i + 1) * width)
+            rows_ref[:, lanes] = sums[i * modules : (i + 1) * modules]
 
 
 def first_kernel(scale, q_hbm, f_hbm, o_ref, f_ref, q_ref, rows_ref, sems):
@@ -82,11 +105,13 @@
 
 def second_kernel(scale, own_ref, q_ref, f_ref, o_ref, rows_ref):
     count = own_ref.shape[0]
+    first = lax.axis_index("rows") % 2 == 0
     mine, pick = lane_masks(f_ref.shape[-1])
-    o_ref[:count] = own_ref[...]
     for i in range(count):
         flatten(both_sides(squares(q_ref[i], mine, pick), f_ref, scale), mine, pick, rows_ref)
-        o_ref[count + i] = rows_ref[...].astype(jnp.bfloat16)
+        own, other = own_ref[i].astype(jnp.float32), rows_ref[...]
+        o_ref[i] = jnp.where(first, own, other).astype(jnp.bfloat16)
+        o_ref[count + i] = jnp.where(first, other, own).astype(jnp.bfloat16)
 
 
 def precondition(queries, factors, modules):
@@ -140,40 +165,34 @@
 
 def scores_direct(queries, train_grads, factors, modules, rows):
     planes = rows // 2
-    plane, odd, low = lax.axis_index("rows") // 2, lax.axis_index("rows") % 2, lax.axis_index("mod") == 0
+    plane, core = lax.axis_index("rows") // 2, lax.axis_index("mod")
     neighbour = send_rows(queries, lambda r: r ^ 1)
     own, tables = precondition(queries, factors, modules)
     pair = precondition_more(own, neighbour, tables, modules)
     far = [named(pair, ("rows", "mod"), lambda i: ((i // 2 + 2) % rows) * 2 + 1 - i % 2)]
     for s in range(2, planes):
         far.append(named(pair, "rows", lambda r, s=s: (r + 2 * s) % rows))
-    far[0] = named(far[0], "mod", lambda c: 1 - c)
-    count = queries.shape[0]
-
-    def products(pieces):
-        part = dot_rows(jnp.concatenate(pieces), train_grads).reshape(len(pieces), 2, count, -1)
-        return jnp.where(odd == 0, part, part[:, ::-1])
-
-    early = products([pair] + far[1:-1])
-    early = jnp.concatenate([early[:1], jnp.zeros_like(early[:1]), early[1:], jnp.zeros_like(early[:1])])
-    early = jnp.stack([early[-p % planes] for p in range(planes)])
-    step = 1
-    while step < planes:
-        early = jnp.where(plane & step == 0, early, jnp.roll(early, step, axis=0))
-        step *= 2
-    half = planes // 2
-    late = products([far[0], far[-1]])
-    place = jnp.arange(half)[:, None, None, None]
-
-    def whole(kept, first):
-        where = place + first
-        kept = jnp.where(where == (plane - 1) % planes, late[:1], kept)
-        kept = jnp.where(where == (plane + 1) % planes, late[1:], kept)
-        return kept.reshape(rows // 2 * count, -1)
-
-    keep = whole(jnp.where(low, early[:half], early[half:]), jnp.where(low, 0, half))
-    give = whole(jnp.where(low, early[half:], early[:half]), jnp.where(low, half, 0))
-    return keep + lax.ppermute(give, "mod", [(0, 1), (1, 0)])
+    back = named(far[0], "mod", lambda c: 1 - c)
+    first = back
+    half, each = planes // 2, pair.shape[0]
+
+    def planes_of(core):
+        at = lax.broadcasted_iota(jnp.int32, (half * each, train_grads.shape[0]), 0)
+        return core * half + at // each
+
+    def place(part, i, s, rest, core):
+        part = jnp.concatenate([part[i * each : (i + 1) * each]] * half)
+        return jnp.where(planes_of(core) == (plane - s) % planes, part, rest)
+
+    early = dot_rows(jnp.concatenate([pair, far[1]]), train_grads)
+    late = dot_rows(jnp.concatenate([first, far[2]]), train_grads)
+
+    def whole(core):
+        rows_early = place(early, 0, 0, jnp.concatenate([early[each:]] * half), core)
+        return place(late, 0, 1, place(late, 1, 3, rows_early, core), core)
+
+    got = lax.ppermute(whole(1 - core), "mod", [(0, 1), (1, 0)])
+    return lax.optimization_barrier(whole(core)) + got
 
 
 def scores_gathered(own, train_grads):

time: 16 us -> 15.9 us (level)
  no operation moved by 1% of the time
where the time goes in v1:
time: 15.9 us; the launch traced here: 15.7 us
  starting transfers between devices  8.5 us (53%)
  waiting for transfers between devices  2.66 us (17%)
  Pallas kernels  2.25 us (14%)
  matrix products  1.41 us (9%)
  other arithmetic  0.86 us (5%)
    ppermute x4, starting transfers between devices, named(): lax.ppermute(x, axes, [(i, target(i)) for i in range(lax.axis_size(axes))])  5.33 us
    ppermute x1, starting transfers between devices, send_rows(): lax.ppermute(x, 'rows', [(r, target(r)) for r in range(lax.axis_size('row...  2.97 us
    pallas_call x1, Pallas kernels, precondition(): pl.pallas_call(functools.partial(first_kernel, scale), out_shape=(pltpu.V...  1.55 us
    dot_general x2, matrix products, dot_rows(): lax.dot_general(ready, train_grads, (((1, 2), (1, 2)), ((), ())), preferr...  1.41 us
    ppermute x4, waiting for transfers between devices, named(): lax.ppermute(x, axes, [(i, target(i)) for i in range(lax.axis_size(axes))])  1.38 us
    ppermute x1, waiting for transfers between devices, scores_direct(): got = lax.ppermute(whole(1 - core), 'mod', [(0, 1), (1, 0)])  0.9 us
    pallas_call x1, Pallas kernels, precondition_more(): pl.pallas_call(functools.partial(second_kernel, scale), out_shape=pltpu.V...  0.7 us
    add x1, other arithmetic, scores_direct(): return lax.optimization_barrier(whole(core)) + got  0.58 us
  transfers between devices with their start and end apart: 6, of which 4 were waited for; matrix products, arithmetic and copies ran while one was open for 5% of the time, Pallas kernels for 10%

profile of v1, /device:TPU:0, one launch (start us, length us, event | category | flops | bytes accessed | tf_op | source)
XLA Modules:
  0.0 15.7 jit_solution(15970202074174482166)
XLA Ops:
  0.0 0.0 copy-start
  0.0 3.0 %collective-permute-start = (bf16[1,4,2304]{2,1,0:T(4,128)(2,1)}, bf16[1,4,2304]{2,1,0:T(4,128)(2,1)S(1)}, u32[]{:S(2)}, u32[]{:S(2)}) collective-permute-start(bf16[1,4,2304]{2,1,0:T(4,128)(2,1)} %q_hbm.1), channel_id=1, source_target_pairs={{0,2},{2,0},{4,6},{6,4},{8,10},{10,8},{12,14},{14,12},{1,3},{3,1},... | collective-permute-start | bytes 55304 | tf_op jit(solution)/shard_map/ppermute | solution.py:159
  3.0 1.5 %precondition_own.1 = (bf16[1,4,2304]{2,1,0:T(4,128)(2,1)S(1)}, f32[4,2,48,48]{3,2,1,0:T(8,128)S(1)}) custom-call(bf16[1,4,2304]{2,1,0:T(4,128)(2,1)} %q_hbm.1, f32[4,2,48,48]{3,2,1,0:T(8,128)} %f_hbm.1), custom_call_target="tpu_custom_call" | custom-call | flops 10616832 | bytes 110592 | tf_op jit(solution)/shard_map/precondition_own/pallas_call | solution.py:120
  4.5 0.4 %collective-permute-done.q_ref = bf16[1,4,2304]{2,1,0:T(4,128)(2,1)S(1)} collective-permute-done((bf16[1,4,2304]{2,1,0:T(4,128)(2,1)}, bf16[1,4,2304]{2,1,0:T(4,128)(2,1)S(1)}, u32[]{:S(2)}, u32[]{:S(2)}) %collective-permute-start) | collective-permute-done | bytes 18464 | tf_op jit(solution)/shard_map/ppermute | solution.py:159
  4.9 0.7 %precondition_neighbour.1 = bf16[2,4,2304]{2,1,0:T(4,128)(2,1)S(1)} custom-call(bf16[1,4,2304]{2,1,0:T(4,128)(2,1)S(1)} %get-tuple-element.7.own_ref, bf16[1,4,2304]{2,1,0:T(4,128)(2,1)S(1)} %collective-permute-done.q_ref, f32[4,2,48,48]{3,2,1,0:T(8,128)S(1)} %get-tuple-element.8.f_ref), custom_call_target="tpu_custom_call" | custom-call | tf_op jit(solution)/shard_map/precondition_neighbour/pallas_call | solution.py:141
  5.6 0.5 %collective-permute-start.1 = (bf16[2,4,2304]{2,1,0:T(4,128)(2,1)S(1)}, bf16[2,4,2304]{2,1,0:T(4,128)(2,1)S(1)}, u32[]{:S(2)}, u32[]{:S(2)}) collective-permute-start(bf16[2,4,2304]{2,1,0:T(4,128)(2,1)S(1)} %precondition_neighbour.1), channel_id=1, source_target_pairs={{0,5},{1,4},{2,7},{3,6},{4,9},{5,8},{6,11},{7,10},{8,13},{9,12},{1... | collective-permute-start | bytes 110600 | tf_op jit(solution)/shard_map/ppermute | solution.py:163
  6.1 2.8 %collective-permute-start.4 = (bf16[2,4,2304]{2,1,0:T(4,128)(2,1)S(1)}, bf16[2,4,2304]{2,1,0:T(4,128)(2,1)S(1)}, u32[]{:S(2)}, u32[]{:S(2)}) collective-permute-start(bf16[2,4,2304]{2,1,0:T(4,128)(2,1)S(1)} %precondition_neighbour.1), channel_id=1, source_target_pairs={{0,8},{2,10},{4,12},{6,14},{8,0},{10,2},{12,4},{14,6},{1,9},{3,11}... | collective-permute-start | bytes 110600 | tf_op jit(solution)/shard_map/ppermute | solution.py:163
  8.9 1.3 %collective-permute-start.3 = (bf16[2,4,2304]{2,1,0:T(4,128)(2,1)S(1)}, bf16[2,4,2304]{2,1,0:T(4,128)(2,1)S(1)}, u32[]{:S(2)}, u32[]{:S(2)}) collective-permute-start(bf16[2,4,2304]{2,1,0:T(4,128)(2,1)S(1)} %precondition_neighbour.1), channel_id=1, source_target_pairs={{0,12},{2,14},{4,0},{6,2},{8,4},{10,6},{12,8},{14,10},{1,13},{3,15... | collective-permute-start | bytes 110600 | tf_op jit(solution)/shard_map/ppermute | solution.py:163
  10.2 0.7 %collective-permute-done.1 = bf16[2,4,2304]{2,1,0:T(4,128)(2,1)S(1)} collective-permute-done((bf16[2,4,2304]{2,1,0:T(4,128)(2,1)S(1)}, bf16[2,4,2304]{2,1,0:T(4,128)(2,1)S(1)}, u32[]{:S(2)}, u32[]{:S(2)}) %collective-permute-start.1) | collective-permute-done | bytes 36896 | tf_op jit(solution)/shard_map/ppermute | solution.py:163
  10.9 0.7 %collective-permute-start.2 = (bf16[2,4,2304]{2,1,0:T(4,128)(2,1)S(1)}, bf16[2,4,2304]{2,1,0:T(4,128)(2,1)S(1)}, u32[]{:S(2)}, u32[]{:S(2)}) collective-permute-start(bf16[2,4,2304]{2,1,0:T(4,128)(2,1)S(1)} %collective-permute-done.1), channel_id=1, source_target_pairs={{0,1},{1,0},{2,3},{3,2},{4,5},{5,4},{6,7},{7,6},{8,9},{9,8},{10,11... | collective-permute-start | bytes 110600 | tf_op jit(solution)/shard_map/ppermute | solution.py:163
  11.6 0.0 collective-permute-done.4
  11.6 0.1 pad_maximum_fusion.1
  11.7 0.0 copy-done
  11.7 0.7 %fusion.7 = f32[4,128]{1,0:T(4,128)S(1)} fusion(bf16[128,4,2304]{2,1,0:T(4,128)(2,1)S(1)} %copy-done, bf16[4,4,2304]{2,1,0:T(4,128)(2,1)S(1)} %pad_maximum_fusion.1), kind=kOutput, calls=%fused_computation.5 | convolution fusion | flops 9437184 | bytes 2435072 | tf_op jit(solution)/shard_map/dot_general | solution.py:153
  12.4 0.7 %collective-permute-done.3 = bf16[2,4,2304]{2,1,0:T(4,128)(2,1)S(1)} collective-permute-done((bf16[2,4,2304]{2,1,0:T(4,128)(2,1)S(1)}, bf16[2,4,2304]{2,1,0:T(4,128)(2,1)S(1)}, u32[]{:S(2)}, u32[]{:S(2)}) %collective-permute-start.3) | collective-permute-done | bytes 36896 | tf_op jit(solution)/shard_map/ppermute | solution.py:163
  13.1 0.0 collective-permute-done.2
  13.1 0.1 pad_maximum_fusion
  13.2 0.7 %fusion.4 = f32[4,128]{1,0:T(4,128)S(1)} fusion(bf16[128,4,2304]{2,1,0:T(4,128)(2,1)S(1)} %copy-done, bf16[4,4,2304]{2,1,0:T(4,128)(2,1)S(1)} %pad_maximum_fusion), kind=kOutput, calls=%fused_computation.4 | convolution fusion | flops 9437184 | bytes 2435072 | tf_op jit(solution)/shard_map/dot_general | solution.py:153
  13.9 0.1 select_select_fusion
  14.0 0.2 %collective-permute-start.5 = (f32[4,128]{1,0:T(4,128)S(1)}, f32[4,128]{1,0:T(4,128)S(1)}, u32[]{:S(2)}, u32[]{:S(2)}) collective-permute-start(f32[4,128]{1,0:T(4,128)S(1)} %select_select_fusion), channel_id=1, source_target_pairs={{0,1},{1,0},{2,3},{3,2},{4,5},{5,4},{6,7},{7,6},{8,9},{9,8},{10,11... | collective-permute-start | bytes 6152 | tf_op jit(solution)/shard_map/ppermute | solution.py:194
  14.2 0.1 select_select_fusion.1
  14.2 0.9 %collective-permute-done.5 = f32[4,128]{1,0:T(4,128)S(1)} collective-permute-done((f32[4,128]{1,0:T(4,128)S(1)}, f32[4,128]{1,0:T(4,128)S(1)}, u32[]{:S(2)}, u32[]{:S(2)}) %collective-permute-start.5) | collective-permute-done | bytes 2080 | tf_op jit(solution)/shard_map/ppermute | solution.py:194
  15.1 0.6 %add.48 = f32[4,128]{1,0:T(4,128)} add(f32[4,128]{1,0:T(4,128)S(1)} %select_select_fusion.1, f32[4,128]{1,0:T(4,128)S(1)} %collective-permute-done.5) | non-fusion elementwise | flops 512 | bytes 6144 | tf_op jit(solution)/shard_map/add | solution.py:195
  (3 shorter events, 0.0 us)
Async XLA Ops:
  0.0 11.7 %copy-start = (bf16[128,4,2304]{2,1,0:T(4,128)(2,1)S(1)}, bf16[128,4,2304]{2,1,0:T(4,128)(2,1)}, u32[]{:S(2)}) copy-start(bf16[128,4,2304]{2,1,0:T(4,128)(2,1)} %param.4) | copy-start | bytes 7077892
  0.0 4.9 %collective-permute-start = (bf16[1,4,2304]{2,1,0:T(4,128)(2,1)}, bf16[1,4,2304]{2,1,0:T(4,128)(2,1)S(1)}, u32[]{:S(2)}, u32[]{:S(2)}) collective-permute-start(bf16[1,4,2304]{2,1,0:T(4,128)(2,1)} %q_hbm.1), channel_id=1, source_target_pairs={{0,2},{2,0},{4,6},{6,4},{8,10},{10,8},{12,14},{14,12},{1,3},{3,1},... | collective-permute-start | bytes 55304 | tf_op jit(solution)/shard_map/ppermute | solution.py:159
  5.6 5.3 %collective-permute-start.1 = (bf16[2,4,2304]{2,1,0:T(4,128)(2,1)S(1)}, bf16[2,4,2304]{2,1,0:T(4,128)(2,1)S(1)}, u32[]{:S(2)}, u32[]{:S(2)}) collective-permute-start(bf16[2,4,2304]{2,1,0:T(4,128)(2,1)S(1)} %precondition_neighbour.1), channel_id=1, source_target_pairs={{0,5},{1,4},{2,7},{3,6},{4,9},{5,8},{6,11},{7,10},{8,13},{9,12},{1... | collective-permute-start | bytes 110600 | tf_op jit(solution)/shard_map/ppermute | solution.py:163
  6.1 5.5 %collective-permute-start.4 = (bf16[2,4,2304]{2,1,0:T(4,128)(2,1)S(1)}, bf16[2,4,2304]{2,1,0:T(4,128)(2,1)S(1)}, u32[]{:S(2)}, u32[]{:S(2)}) collective-permute-start(bf16[2,4,2304]{2,1,0:T(4,128)(2,1)S(1)} %precondition_neighbour.1), channel_id=1, source_target_pairs={{0,8},{2,10},{4,12},{6,14},{8,0},{10,2},{12,4},{14,6},{1,9},{3,11}... | collective-permute-start | bytes 110600 | tf_op jit(solution)/shard_map/ppermute | solution.py:163
  8.9 4.2 %collective-permute-start.3 = (bf16[2,4,2304]{2,1,0:T(4,128)(2,1)S(1)}, bf16[2,4,2304]{2,1,0:T(4,128)(2,1)S(1)}, u32[]{:S(2)}, u32[]{:S(2)}) collective-permute-start(bf16[2,4,2304]{2,1,0:T(4,128)(2,1)S(1)} %precondition_neighbour.1), channel_id=1, source_target_pairs={{0,12},{2,14},{4,0},{6,2},{8,4},{10,6},{12,8},{14,10},{1,13},{3,15... | collective-permute-start | bytes 110600 | tf_op jit(solution)/shard_map/ppermute | solution.py:163
  10.9 2.2 %collective-permute-start.2 = (bf16[2,4,2304]{2,1,0:T(4,128)(2,1)S(1)}, bf16[2,4,2304]{2,1,0:T(4,128)(2,1)S(1)}, u32[]{:S(2)}, u32[]{:S(2)}) collective-permute-start(bf16[2,4,2304]{2,1,0:T(4,128)(2,1)S(1)} %collective-permute-done.1), channel_id=1, source_target_pairs={{0,1},{1,0},{2,3},{3,2},{4,5},{5,4},{6,7},{7,6},{8,9},{9,8},{10,11... | collective-permute-start | bytes 110600 | tf_op jit(solution)/shard_map/ppermute | solution.py:163
  14.0 1.2 %collective-permute-start.5 = (f32[4,128]{1,0:T(4,128)S(1)}, f32[4,128]{1,0:T(4,128)S(1)}, u32[]{:S(2)}, u32[]{:S(2)}) collective-permute-start(f32[4,128]{1,0:T(4,128)S(1)} %select_select_fusion), channel_id=1, source_target_pairs={{0,1},{1,0},{2,3},{3,2},{4,5},{5,4},{6,7},{7,6},{8,9},{9,8},{10,11... | collective-permute-start | bytes 6152 | tf_op jit(solution)/shard_map/ppermute | solution.py:194

commit v2 on v1

--- a/solution.py
+++ b/solution.py
@@ -10,7 +10,7 @@
 from jax.sharding import PartitionSpec as P
 
 
-DIRECT_PLANES = 4
+DIRECT_GROUPS = 4
 
 HI = lax.Precision.HIGHEST
 NT = (((1,), (1,)), ((), ()))
@@ -41,15 +41,27 @@
     return lax.dot_general(spread, pick, NT, preferred_element_type=jnp.float32)
 
 
+def split(x):
+    parts = []
+    for _ in range(3):
+        parts.append(x.astype(jnp.bfloat16))
+        x = x - parts[-1].astype(jnp.float32)
+    return parts
+
+
 def both_sides(square, f_ref, scale):
-    proj = f_ref.shape[-1]
-    both = []
-    rights = [lax.dot_general(
-        square[m * proj : (m + 1) * proj], f_ref[m, 1], NN,
-        precision=HI, preferred_element_type=jnp.float32) for m in range(f_ref.shape[0])]
-    for m in range(f_ref.shape[0]):
-        both.append(lax.dot_general(
-            f_ref[m, 0], rights[m], NN, precision=HI, preferred_element_type=jnp.float32))
+    modules, proj = f_ref.shape[0], f_ref.shape[-1]
+    square = square.astype(jnp.bfloat16)
+    rights = []
+    for m in range(modules):
+        rows = square[m * proj : (m + 1) * proj]
+        rights.append(sum(
+            lax.dot_general(rows, part, NN, preferred_element_type=jnp.float32)
+            for part in split(f_ref[m, 1])))
+    both = [
+        lax.dot_general(f_ref[m, 0], rights[m], NN, precision=HI, preferred_element_type=jnp.float32)
+        for m in range(modules)
+    ]
     return (jnp.concatenate(both, axis=0) / scale).astype(jnp.bfloat16)
 
 
@@ -105,7 +117,7 @@
 
 def second_kernel(scale, own_ref, q_ref, f_ref, o_ref, rows_ref):
     count = own_ref.shape[0]
-    first = lax.axis_index("rows") % 2 == 0
+    first = lax.axis_index("rows") < lax.axis_size("rows") // 2
     mine, pick = lane_masks(f_ref.shape[-1])
     for i in range(count):
         flatten(both_sides(squares(q_ref[i], mine, pick), f_ref, scale), mine, pick, rows_ref)
@@ -164,32 +176,33 @@
 
 
 def scores_direct(queries, train_grads, factors, modules, rows):
-    planes = rows // 2
-    plane, core = lax.axis_index("rows") // 2, lax.axis_index("mod")
-    neighbour = send_rows(queries, lambda r: r ^ 1)
+    groups = rows // 2
+    group, core = lax.axis_index("rows") % groups, lax.axis_index("mod")
+    neighbour = send_rows(queries, lambda r: (r + groups) % rows)
     own, tables = precondition(queries, factors, modules)
     pair = precondition_more(own, neighbour, tables, modules)
-    far = [named(pair, ("rows", "mod"), lambda i: ((i // 2 + 2) % rows) * 2 + 1 - i % 2)]
-    for s in range(2, planes):
-        far.append(named(pair, "rows", lambda r, s=s: (r + 2 * s) % rows))
+
+    def shifted(r, s):
+        return r // groups * groups + (r + s) % groups
+
+    far = [named(pair, ("rows", "mod"), lambda i: shifted(i // 2, 1) * 2 + 1 - i % 2)]
+    for s in range(2, groups):
+        far.append(named(pair, "rows", lambda r, s=s: shifted(r, s)))
     back = named(far[0], "mod", lambda c: 1 - c)
-    first = back
-    half, each = planes // 2, pair.shape[0]
-
-    def planes_of(core):
-        at = lax.broadcasted_iota(jnp.int32, (half * each, train_grads.shape[0]), 0)
-        return core * half + at // each
+    count = queries.shape[0]
+    owner = lax.broadcasted_iota(jnp.int32, (groups * count, train_grads.shape[0]), 0) // count
 
     def place(part, i, s, rest, core):
-        part = jnp.concatenate([part[i * each : (i + 1) * each]] * half)
-        return jnp.where(planes_of(core) == (plane - s) % planes, part, rest)
+        part = part[2 * i * count : 2 * (i + 1) * count]
+        part = jnp.concatenate([jnp.where(core == 0, part[:count], part[count:])] * groups)
+        return jnp.where(owner == (group - s) % groups, part, rest)
 
     early = dot_rows(jnp.concatenate([pair, far[1]]), train_grads)
-    late = dot_rows(jnp.concatenate([first, far[2]]), train_grads)
+    late = dot_rows(jnp.concatenate([back, far[2]]), train_grads)
 
     def whole(core):
-        rows_early = place(early, 0, 0, jnp.concatenate([early[each:]] * half), core)
-        return place(late, 0, 1, place(late, 1, 3, rows_early, core), core)
+        scores = place(early, 1, 2, place(early, 0, 0, 0.0, core), core)
+        return place(late, 0, 1, place(late, 1, 3, scores, core), core)
 
     got = lax.ppermute(whole(1 - core), "mod", [(0, 1), (1, 0)])
     return lax.optimization_barrier(whole(core)) + got
@@ -201,7 +214,7 @@
 
 
 def goes_direct(rows, cores):
-    return cores == 2 and rows == 2 * DIRECT_PLANES
+    return cores == 2 and rows == 2 * DIRECT_GROUPS
 
 
 def shards(queries, train_grads, factors):

time: 15.9 us -> 15.6 us (0.981)
  starting transfers between devices: 8.5 us -> 8.05 us
  waiting for transfers between devices: 2.66 us -> 3 us
    ppermute x4, starting transfers between devices: 5.33 us -> 3.81 us  [named(): lax.ppermute(x, axes, [(i, target(i)) for i in range(lax.axis_size(axes))])]
    ppermute x1, starting transfers between devices: 2.97 us -> 4.06 us  [send_rows(): lax.ppermute(x, 'rows', [(r, target(r)) for r in range(lax.axis_size('row...]
    ppermute x4, waiting for transfers between devices: 1.38 us -> 1.56 us  [named(): lax.ppermute(x, axes, [(i, target(i)) for i in range(lax.axis_size(axes))])]
where the time goes in v2:
time: 15.6 us; the launch traced here: 15.5 us
  starting transfers between devices  8.05 us (52%)
  waiting for transfers between devices  3 us (19%)
  Pallas kernels  2.23 us (14%)
  matrix products  1.41 us (9%)
  other arithmetic  0.71 us (5%)
    ppermute x1, starting transfers between devices, send_rows(): lax.ppermute(x, 'rows', [(r, target(r)) for r in range(lax.axis_size('row...  4.06 us
    ppermute x4, starting transfers between devices, named(): lax.ppermute(x, axes, [(i, target(i)) for i in range(lax.axis_size(axes))])  3.81 us
    ppermute x4, waiting for transfers between devices, named(): lax.ppermute(x, axes, [(i, target(i)) for i in range(lax.axis_size(axes))])  1.56 us
    pallas_call x1, Pallas kernels, precondition(): pl.pallas_call(functools.partial(first_kernel, scale), out_shape=(pltpu.V...  1.54 us
    dot_general x2, matrix products, dot_rows(): lax.dot_general(ready, train_grads, (((1, 2), (1, 2)), ((), ())), preferr...  1.41 us
    ppermute x1, waiting for transfers between devices, scores_direct(): got = lax.ppermute(whole(1 - core), 'mod', [(0, 1), (1, 0)])  1.04 us
    pallas_call x1, Pallas kernels, precondition_more(): pl.pallas_call(functools.partial(second_kernel, scale), out_shape=pltpu.V...  0.68 us
    add x1, other arithmetic, scores_direct(): return lax.optimization_barrier(whole(core)) + got  0.58 us
  transfers between devices with their start and end apart: 6, of which 4 were waited for; matrix products, arithmetic and copies ran while one was open for 5% of the time, Pallas kernels for 10%

profile of v2, /device:TPU:0, one launch (start us, length us, event | category | flops | bytes accessed | tf_op | source)
XLA Modules:
  0.0 15.5 jit_solution(18422707797312856756)
XLA Ops:
  0.0 0.0 copy-start
  0.0 4.1 %collective-permute-start = (bf16[1,4,2304]{2,1,0:T(4,128)(2,1)}, bf16[1,4,2304]{2,1,0:T(4,128)(2,1)S(1)}, u32[]{:S(2)}, u32[]{:S(2)}) collective-permute-start(bf16[1,4,2304]{2,1,0:T(4,128)(2,1)} %q_hbm.1), channel_id=1, source_target_pairs={{0,8},{2,10},{4,12},{6,14},{8,0},{10,2},{12,4},{14,6},{1,9},{3,11}... | collective-permute-start | bytes 55304 | tf_op jit(solution)/shard_map/ppermute | solution.py:171
  4.1 1.5 %precondition_own.1 = (bf16[1,4,2304]{2,1,0:T(4,128)(2,1)S(1)}, f32[4,2,48,48]{3,2,1,0:T(8,128)S(1)}) custom-call(bf16[1,4,2304]{2,1,0:T(4,128)(2,1)} %q_hbm.1, f32[4,2,48,48]{3,2,1,0:T(8,128)} %f_hbm.1), custom_call_target="tpu_custom_call" | custom-call | flops 10616832 | bytes 110592 | tf_op jit(solution)/shard_map/precondition_own/pallas_call | solution.py:132
  5.6 0.4 %collective-permute-done.q_ref = bf16[1,4,2304]{2,1,0:T(4,128)(2,1)S(1)} collective-permute-done((bf16[1,4,2304]{2,1,0:T(4,128)(2,1)}, bf16[1,4,2304]{2,1,0:T(4,128)(2,1)S(1)}, u32[]{:S(2)}, u32[]{:S(2)}) %collective-permute-start) | collective-permute-done | bytes 18464 | tf_op jit(solution)/shard_map/ppermute | solution.py:171
  6.0 0.7 %precondition_neighbour.1 = bf16[2,4,2304]{2,1,0:T(4,128)(2,1)S(1)} custom-call(bf16[1,4,2304]{2,1,0:T(4,128)(2,1)S(1)} %get-tuple-element.7.own_ref, bf16[1,4,2304]{2,1,0:T(4,128)(2,1)S(1)} %collective-permute-done.q_ref, f32[4,2,48,48]{3,2,1,0:T(8,128)S(1)} %get-tuple-element.8.f_ref), custom_call_target="tpu_custom_call" | custom-call | tf_op jit(solution)/shard_map/precondition_neighbour/pallas_call | solution.py:153
  6.7 0.3 %collective-permute-start.1 = (bf16[2,4,2304]{2,1,0:T(4,128)(2,1)S(1)}, bf16[2,4,2304]{2,1,0:T(4,128)(2,1)S(1)}, u32[]{:S(2)}, u32[]{:S(2)}) collective-permute-start(bf16[2,4,2304]{2,1,0:T(4,128)(2,1)S(1)} %precondition_neighbour.1), channel_id=1, source_target_pairs={{0,3},{1,2},{2,5},{3,4},{4,7},{5,6},{6,1},{7,0},{8,11},{9,10},{10,... | collective-permute-start | bytes 110600 | tf_op jit(solution)/shard_map/ppermute | solution.py:175
  7.0 1.7 %collective-permute-start.4 = (bf16[2,4,2304]{2,1,0:T(4,128)(2,1)S(1)}, bf16[2,4,2304]{2,1,0:T(4,128)(2,1)S(1)}, u32[]{:S(2)}, u32[]{:S(2)}) collective-permute-start(bf16[2,4,2304]{2,1,0:T(4,128)(2,1)S(1)} %precondition_neighbour.1), channel_id=1, source_target_pairs={{0,4},{2,6},{4,0},{6,2},{8,12},{10,14},{12,8},{14,10},{1,5},{3,7},... | collective-permute-start | bytes 110600 | tf_op jit(solution)/shard_map/ppermute | solution.py:175
  8.8 1.4 %collective-permute-start.3 = (bf16[2,4,2304]{2,1,0:T(4,128)(2,1)S(1)}, bf16[2,4,2304]{2,1,0:T(4,128)(2,1)S(1)}, u32[]{:S(2)}, u32[]{:S(2)}) collective-permute-start(bf16[2,4,2304]{2,1,0:T(4,128)(2,1)S(1)} %precondition_neighbour.1), channel_id=1, source_target_pairs={{0,6},{2,0},{4,2},{6,4},{8,14},{10,8},{12,10},{14,12},{1,7},{3,1},... | collective-permute-start | bytes 110600 | tf_op jit(solution)/shard_map/ppermute | solution.py:175
  10.2 0.8 %collective-permute-done.1 = bf16[2,4,2304]{2,1,0:T(4,128)(2,1)S(1)} collective-permute-done((bf16[2,4,2304]{2,1,0:T(4,128)(2,1)S(1)}, bf16[2,4,2304]{2,1,0:T(4,128)(2,1)S(1)}, u32[]{:S(2)}, u32[]{:S(2)}) %collective-permute-start.1) | collective-permute-done | bytes 36896 | tf_op jit(solution)/shard_map/ppermute | solution.py:175
  11.0 0.3 %collective-permute-start.2 = (bf16[2,4,2304]{2,1,0:T(4,128)(2,1)S(1)}, bf16[2,4,2304]{2,1,0:T(4,128)(2,1)S(1)}, u32[]{:S(2)}, u32[]{:S(2)}) collective-permute-start(bf16[2,4,2304]{2,1,0:T(4,128)(2,1)S(1)} %collective-permute-done.1), channel_id=1, source_target_pairs={{0,1},{1,0},{2,3},{3,2},{4,5},{5,4},{6,7},{7,6},{8,9},{9,8},{10,11... | collective-permute-start | bytes 110600 | tf_op jit(solution)/shard_map/ppermute | solution.py:175
  11.4 0.0 collective-permute-done.4
  11.4 0.1 pad_maximum_fusion.1
  11.4 0.0 copy-done
  11.4 0.7 %fusion.7 = f32[4,128]{1,0:T(4,128)S(1)} fusion(bf16[128,4,2304]{2,1,0:T(4,128)(2,1)S(1)} %copy-done, bf16[4,4,2304]{2,1,0:T(4,128)(2,1)S(1)} %pad_maximum_fusion.1), kind=kOutput, calls=%fused_computation.5 | convolution fusion | flops 9437184 | bytes 2435072 | tf_op jit(solution)/shard_map/dot_general | solution.py:165
  12.1 0.7 %collective-permute-done.3 = bf16[2,4,2304]{2,1,0:T(4,128)(2,1)S(1)} collective-permute-done((bf16[2,4,2304]{2,1,0:T(4,128)(2,1)S(1)}, bf16[2,4,2304]{2,1,0:T(4,128)(2,1)S(1)}, u32[]{:S(2)}, u32[]{:S(2)}) %collective-permute-start.3) | collective-permute-done | bytes 36896 | tf_op jit(solution)/shard_map/ppermute | solution.py:175
  12.8 0.0 collective-permute-done.2
  12.8 0.1 pad_maximum_fusion
  12.9 0.7 %fusion.4 = f32[4,128]{1,0:T(4,128)S(1)} fusion(bf16[128,4,2304]{2,1,0:T(4,128)(2,1)S(1)} %copy-done, bf16[4,4,2304]{2,1,0:T(4,128)(2,1)S(1)} %pad_maximum_fusion), kind=kOutput, calls=%fused_computation.4 | convolution fusion | flops 9437184 | bytes 2435072 | tf_op jit(solution)/shard_map/dot_general | solution.py:165
  13.6 0.2 %collective-permute-start.5 = (f32[4,128]{1,0:T(4,128)S(1)}, f32[4,128]{1,0:T(4,128)S(1)}, u32[]{:S(2)}, u32[]{:S(2)}) collective-permute-start(f32[4,128]{1,0:T(4,128)S(1)} %select_select_fusion), channel_id=1, source_target_pairs={{0,1},{1,0},{2,3},{3,2},{4,5},{5,4},{6,7},{7,6},{8,9},{9,8},{10,11... | collective-permute-start | bytes 6152 | tf_op jit(solution)/shard_map/ppermute | solution.py:207
  13.8 1.0 %collective-permute-done.5 = f32[4,128]{1,0:T(4,128)S(1)} collective-permute-done((f32[4,128]{1,0:T(4,128)S(1)}, f32[4,128]{1,0:T(4,128)S(1)}, u32[]{:S(2)}, u32[]{:S(2)}) %collective-permute-start.5) | collective-permute-done | bytes 2080 | tf_op jit(solution)/shard_map/ppermute | solution.py:207
  14.9 0.6 %add.33 = f32[4,128]{1,0:T(4,128)} add(f32[4,128]{1,0:T(4,128)S(1)} %select_select_fusion.1, f32[4,128]{1,0:T(4,128)S(1)} %collective-permute-done.5) | non-fusion elementwise | flops 512 | bytes 6144 | tf_op jit(solution)/shard_map/add | solution.py:208
  (3 shorter events, 0.0 us)
Async XLA Ops:
  0.0 11.4 %copy-start = (bf16[128,4,2304]{2,1,0:T(4,128)(2,1)S(1)}, bf16[128,4,2304]{2,1,0:T(4,128)(2,1)}, u32[]{:S(2)}) copy-start(bf16[128,4,2304]{2,1,0:T(4,128)(2,1)} %param.4) | copy-start | bytes 7077892
  0.0 6.0 %collective-permute-start = (bf16[1,4,2304]{2,1,0:T(4,128)(2,1)}, bf16[1,4,2304]{2,1,0:T(4,128)(2,1)S(1)}, u32[]{:S(2)}, u32[]{:S(2)}) collective-permute-start(bf16[1,4,2304]{2,1,0:T(4,128)(2,1)} %q_hbm.1), channel_id=1, source_target_pairs={{0,8},{2,10},{4,12},{6,14},{8,0},{10,2},{12,4},{14,6},{1,9},{3,11}... | collective-permute-start | bytes 55304 | tf_op jit(solution)/shard_map/ppermute | solution.py:171
  6.7 4.3 %collective-permute-start.1 = (bf16[2,4,2304]{2,1,0:T(4,128)(2,1)S(1)}, bf16[2,4,2304]{2,1,0:T(4,128)(2,1)S(1)}, u32[]{:S(2)}, u32[]{:S(2)}) collective-permute-start(bf16[2,4,2304]{2,1,0:T(4,128)(2,1)S(1)} %precondition_neighbour.1), channel_id=1, source_target_pairs={{0,3},{1,2},{2,5},{3,4},{4,7},{5,6},{6,1},{7,0},{8,11},{9,10},{10,... | collective-permute-start | bytes 110600 | tf_op jit(solution)/shard_map/ppermute | solution.py:175
  7.0 4.3 %collective-permute-start.4 = (bf16[2,4,2304]{2,1,0:T(4,128)(2,1)S(1)}, bf16[2,4,2304]{2,1,0:T(4,128)(2,1)S(1)}, u32[]{:S(2)}, u32[]{:S(2)}) collective-permute-start(bf16[2,4,2304]{2,1,0:T(4,128)(2,1)S(1)} %precondition_neighbour.1), channel_id=1, source_target_pairs={{0,4},{2,6},{4,0},{6,2},{8,12},{10,14},{12,8},{14,10},{1,5},{3,7},... | collective-permute-start | bytes 110600 | tf_op jit(solution)/shard_map/ppermute | solution.py:175
  8.8 4.1 %collective-permute-start.3 = (bf16[2,4,2304]{2,1,0:T(4,128)(2,1)S(1)}, bf16[2,4,2304]{2,1,0:T(4,128)(2,1)S(1)}, u32[]{:S(2)}, u32[]{:S(2)}) collective-permute-start(bf16[2,4,2304]{2,1,0:T(4,128)(2,1)S(1)} %precondition_neighbour.1), channel_id=1, source_target_pairs={{0,6},{2,0},{4,2},{6,4},{8,14},{10,8},{12,10},{14,12},{1,7},{3,1},... | collective-permute-start | bytes 110600 | tf_op jit(solution)/shard_map/ppermute | solution.py:175
  11.0 1.8 %collective-permute-start.2 = (bf16[2,4,2304]{2,1,0:T(4,128)(2,1)S(1)}, bf16[2,4,2304]{2,1,0:T(4,128)(2,1)S(1)}, u32[]{:S(2)}, u32[]{:S(2)}) collective-permute-start(bf16[2,4,2304]{2,1,0:T(4,128)(2,1)S(1)} %collective-permute-done.1), channel_id=1, source_target_pairs={{0,1},{1,0},{2,3},{3,2},{4,5},{5,4},{6,7},{7,6},{8,9},{9,8},{10,11... | collective-permute-start | bytes 110600 | tf_op jit(solution)/shard_map/ppermute | solution.py:175
  13.6 1.2 %collective-permute-start.5 = (f32[4,128]{1,0:T(4,128)S(1)}, f32[4,128]{1,0:T(4,128)S(1)}, u32[]{:S(2)}, u32[]{:S(2)}) collective-permute-start(f32[4,128]{1,0:T(4,128)S(1)} %select_select_fusion), channel_id=1, source_target_pairs={{0,1},{1,0},{2,3},{3,2},{4,5},{5,4},{6,7},{7,6},{8,9},{9,8},{10,11... | collective-permute-start | bytes 6152 | tf_op jit(solution)/shard_map/ppermute | solution.py:207

commit v3 on v2

--- a/solution.py
+++ b/solution.py
@@ -117,13 +117,12 @@
 
 def second_kernel(scale, own_ref, q_ref, f_ref, o_ref, rows_ref):
     count = own_ref.shape[0]
-    first = lax.axis_index("rows") < lax.axis_size("rows") // 2
+    place = jnp.where(lax.axis_index("rows") < lax.axis_size("rows") // 2, 0, count)
     mine, pick = lane_masks(f_ref.shape[-1])
     for i in range(count):
+        o_ref[place + i] = own_ref[i]
         flatten(both_sides(squares(q_ref[i], mine, pick), f_ref, scale), mine, pick, rows_ref)
-        own, other = own_ref[i].astype(jnp.float32), rows_ref[...]
-        o_ref[i] = jnp.where(first, own, other).astype(jnp.bfloat16)
-        o_ref[count + i] = jnp.where(first, other, own).astype(jnp.bfloat16)
+        o_ref[count - place + i] = rows_ref[...].astype(jnp.bfloat16)
 
 
 def precondition(queries, factors, modules):

time: 15.6 us -> 15.6 us (level)
  no operation moved by 1% of the time
where the time goes in v3:
time: 15.6 us; the launch traced here: 15.4 us
  starting transfers between devices  8.05 us (52%)
  waiting for transfers between devices  3 us (19%)
  Pallas kernels  2.22 us (14%)
  matrix products  1.41 us (9%)
  other arithmetic  0.71 us (5%)
    ppermute x1, starting transfers between devices, send_rows(): lax.ppermute(x, 'rows', [(r, target(r)) for r in range(lax.axis_size('row...  4.06 us
    ppermute x4, starting transfers between devices, named(): lax.ppermute(x, axes, [(i, target(i)) for i in range(lax.axis_size(axes))])  3.81 us
    ppermute x4, waiting for transfers between devices, named(): lax.ppermute(x, axes, [(i, target(i)) for i in range(lax.axis_size(axes))])  1.56 us
    pallas_call x1, Pallas kernels, precondition(): pl.pallas_call(functools.partial(first_kernel, scale), out_shape=(pltpu.V...  1.54 us
    dot_general x2, matrix products, dot_rows(): lax.dot_general(ready, train_grads, (((1, 2), (1, 2)), ((), ())), preferr...  1.41 us
    ppermute x1, waiting for transfers between devices, scores_direct(): got = lax.ppermute(whole(1 - core), 'mod', [(0, 1), (1, 0)])  1.04 us
    pallas_call x1, Pallas kernels, precondition_more(): pl.pallas_call(functools.partial(second_kernel, scale), out_shape=pltpu.V...  0.68 us
    add x1, other arithmetic, scores_direct(): return lax.optimization_barrier(whole(core)) + got  0.58 us
  transfers between devices with their start and end apart: 6, of which 4 were waited for; matrix products, arithmetic and copies ran while one was open for 5% of the time, Pallas kernels for 10%

profile of v3, /device:TPU:0, one launch (start us, length us, event | category | flops | bytes accessed | tf_op | source)
XLA Modules:
  0.0 15.4 jit_solution(9396187986084602821)
XLA Ops:
  0.0 0.0 copy-start
  0.0 4.1 %collective-permute-start = (bf16[1,4,2304]{2,1,0:T(4,128)(2,1)}, bf16[1,4,2304]{2,1,0:T(4,128)(2,1)S(1)}, u32[]{:S(2)}, u32[]{:S(2)}) collective-permute-start(bf16[1,4,2304]{2,1,0:T(4,128)(2,1)} %q_hbm.1), channel_id=1, source_target_pairs={{0,8},{2,10},{4,12},{6,14},{8,0},{10,2},{12,4},{14,6},{1,9},{3,11}... | collective-permute-start | bytes 55304 | tf_op jit(solution)/shard_map/ppermute | solution.py:170
  4.1 1.5 %precondition_own.1 = (bf16[1,4,2304]{2,1,0:T(4,128)(2,1)S(1)}, f32[4,2,48,48]{3,2,1,0:T(8,128)S(1)}) custom-call(bf16[1,4,2304]{2,1,0:T(4,128)(2,1)} %q_hbm.1, f32[4,2,48,48]{3,2,1,0:T(8,128)} %f_hbm.1), custom_call_target="tpu_custom_call" | custom-call | flops 10616832 | bytes 110592 | tf_op jit(solution)/shard_map/precondition_own/pallas_call | solution.py:131
  5.6 0.4 %collective-permute-done.q_ref = bf16[1,4,2304]{2,1,0:T(4,128)(2,1)S(1)} collective-permute-done((bf16[1,4,2304]{2,1,0:T(4,128)(2,1)}, bf16[1,4,2304]{2,1,0:T(4,128)(2,1)S(1)}, u32[]{:S(2)}, u32[]{:S(2)}) %collective-permute-start) | collective-permute-done | bytes 18464 | tf_op jit(solution)/shard_map/ppermute | solution.py:170
  6.0 0.7 %precondition_neighbour.1 = bf16[2,4,2304]{2,1,0:T(4,128)(2,1)S(1)} custom-call(bf16[1,4,2304]{2,1,0:T(4,128)(2,1)S(1)} %get-tuple-element.7.own_ref, bf16[1,4,2304]{2,1,0:T(4,128)(2,1)S(1)} %collective-permute-done.q_ref, f32[4,2,48,48]{3,2,1,0:T(8,128)S(1)} %get-tuple-element.8.f_ref), custom_call_target="tpu_custom_call" | custom-call | tf_op jit(solution)/shard_map/precondition_neighbour/pallas_call | solution.py:152
  6.7 0.3 %collective-permute-start.1 = (bf16[2,4,2304]{2,1,0:T(4,128)(2,1)S(1)}, bf16[2,4,2304]{2,1,0:T(4,128)(2,1)S(1)}, u32[]{:S(2)}, u32[]{:S(2)}) collective-permute-start(bf16[2,4,2304]{2,1,0:T(4,128)(2,1)S(1)} %precondition_neighbour.1), channel_id=1, source_target_pairs={{0,3},{1,2},{2,5},{3,4},{4,7},{5,6},{6,1},{7,0},{8,11},{9,10},{10,... | collective-permute-start | bytes 110600 | tf_op jit(solution)/shard_map/ppermute | solution.py:174
  7.0 1.7 %collective-permute-start.4 = (bf16[2,4,2304]{2,1,0:T(4,128)(2,1)S(1)}, bf16[2,4,2304]{2,1,0:T(4,128)(2,1)S(1)}, u32[]{:S(2)}, u32[]{:S(2)}) collective-permute-start(bf16[2,4,2304]{2,1,0:T(4,128)(2,1)S(1)} %precondition_neighbour.1), channel_id=1, source_target_pairs={{0,4},{2,6},{4,0},{6,2},{8,12},{10,14},{12,8},{14,10},{1,5},{3,7},... | collective-permute-start | bytes 110600 | tf_op jit(solution)/shard_map/ppermute | solution.py:174
  8.7 1.4 %collective-permute-start.3 = (bf16[2,4,2304]{2,1,0:T(4,128)(2,1)S(1)}, bf16[2,4,2304]{2,1,0:T(4,128)(2,1)S(1)}, u32[]{:S(2)}, u32[]{:S(2)}) collective-permute-start(bf16[2,4,2304]{2,1,0:T(4,128)(2,1)S(1)} %precondition_neighbour.1), channel_id=1, source_target_pairs={{0,6},{2,0},{4,2},{6,4},{8,14},{10,8},{12,10},{14,12},{1,7},{3,1},... | collective-permute-start | bytes 110600 | tf_op jit(solution)/shard_map/ppermute | solution.py:174
  10.2 0.8 %collective-permute-done.1 = bf16[2,4,2304]{2,1,0:T(4,128)(2,1)S(1)} collective-permute-done((bf16[2,4,2304]{2,1,0:T(4,128)(2,1)S(1)}, bf16[2,4,2304]{2,1,0:T(4,128)(2,1)S(1)}, u32[]{:S(2)}, u32[]{:S(2)}) %collective-permute-start.1) | collective-permute-done | bytes 36896 | tf_op jit(solution)/shard_map/ppermute | solution.py:174
  11.0 0.3 %collective-permute-start.2 = (bf16[2,4,2304]{2,1,0:T(4,128)(2,1)S(1)}, bf16[2,4,2304]{2,1,0:T(4,128)(2,1)S(1)}, u32[]{:S(2)}, u32[]{:S(2)}) collective-permute-start(bf16[2,4,2304]{2,1,0:T(4,128)(2,1)S(1)} %collective-permute-done.1), channel_id=1, source_target_pairs={{0,1},{1,0},{2,3},{3,2},{4,5},{5,4},{6,7},{7,6},{8,9},{9,8},{10,11... | collective-permute-start | bytes 110600 | tf_op jit(solution)/shard_map/ppermute | solution.py:174
  11.3 0.0 collective-permute-done.4
  11.3 0.1 pad_maximum_fusion.1
  11.4 0.0 copy-done
  11.4 0.7 %fusion.7 = f32[4,128]{1,0:T(4,128)S(1)} fusion(bf16[128,4,2304]{2,1,0:T(4,128)(2,1)S(1)} %copy-done, bf16[4,4,2304]{2,1,0:T(4,128)(2,1)S(1)} %pad_maximum_fusion.1), kind=kOutput, calls=%fused_computation.5 | convolution fusion | flops 9437184 | bytes 2435072 | tf_op jit(solution)/shard_map/dot_general | solution.py:164
  12.1 0.7 %collective-permute-done.3 = bf16[2,4,2304]{2,1,0:T(4,128)(2,1)S(1)} collective-permute-done((bf16[2,4,2304]{2,1,0:T(4,128)(2,1)S(1)}, bf16[2,4,2304]{2,1,0:T(4,128)(2,1)S(1)}, u32[]{:S(2)}, u32[]{:S(2)}) %collective-permute-start.3) | collective-permute-done | bytes 36896 | tf_op jit(solution)/shard_map/ppermute | solution.py:174
  12.8 0.0 collective-permute-done.2
  12.8 0.1 pad_maximum_fusion
  12.9 0.7 %fusion.4 = f32[4,128]{1,0:T(4,128)S(1)} fusion(bf16[128,4,2304]{2,1,0:T(4,128)(2,1)S(1)} %copy-done, bf16[4,4,2304]{2,1,0:T(4,128)(2,1)S(1)} %pad_maximum_fusion), kind=kOutput, calls=%fused_computation.4 | convolution fusion | flops 9437184 | bytes 2435072 | tf_op jit(solution)/shard_map/dot_general | solution.py:164
  13.6 0.2 %collective-permute-start.5 = (f32[4,128]{1,0:T(4,128)S(1)}, f32[4,128]{1,0:T(4,128)S(1)}, u32[]{:S(2)}, u32[]{:S(2)}) collective-permute-start(f32[4,128]{1,0:T(4,128)S(1)} %select_select_fusion), channel_id=1, source_target_pairs={{0,1},{1,0},{2,3},{3,2},{4,5},{5,4},{6,7},{7,6},{8,9},{9,8},{10,11... | collective-permute-start | bytes 6152 | tf_op jit(solution)/shard_map/ppermute | solution.py:206
  13.8 1.0 %collective-permute-done.5 = f32[4,128]{1,0:T(4,128)S(1)} collective-permute-done((f32[4,128]{1,0:T(4,128)S(1)}, f32[4,128]{1,0:T(4,128)S(1)}, u32[]{:S(2)}, u32[]{:S(2)}) %collective-permute-start.5) | collective-permute-done | bytes 2080 | tf_op jit(solution)/shard_map/ppermute | solution.py:206
  14.9 0.6 %add.33 = f32[4,128]{1,0:T(4,128)} add(f32[4,128]{1,0:T(4,128)S(1)} %select_select_fusion.1, f32[4,128]{1,0:T(4,128)S(1)} %collective-permute-done.5) | non-fusion elementwise | flops 512 | bytes 6144 | tf_op jit(solution)/shard_map/add | solution.py:207
  (3 shorter events, 0.0 us)
Async XLA Ops:
  0.0 11.4 %copy-start = (bf16[128,4,2304]{2,1,0:T(4,128)(2,1)S(1)}, bf16[128,4,2304]{2,1,0:T(4,128)(2,1)}, u32[]{:S(2)}) copy-start(bf16[128,4,2304]{2,1,0:T(4,128)(2,1)} %param.4) | copy-start | bytes 7077892
  0.0 6.0 %collective-permute-start = (bf16[1,4,2304]{2,1,0:T(4,128)(2,1)}, bf16[1,4,2304]{2,1,0:T(4,128)(2,1)S(1)}, u32[]{:S(2)}, u32[]{:S(2)}) collective-permute-start(bf16[1,4,2304]{2,1,0:T(4,128)(2,1)} %q_hbm.1), channel_id=1, source_target_pairs={{0,8},{2,10},{4,12},{6,14},{8,0},{10,2},{12,4},{14,6},{1,9},{3,11}... | collective-permute-start | bytes 55304 | tf_op jit(solution)/shard_map/ppermute | solution.py:170
  6.7 4.3 %collective-permute-start.1 = (bf16[2,4,2304]{2,1,0:T(4,128)(2,1)S(1)}, bf16[2,4,2304]{2,1,0:T(4,128)(2,1)S(1)}, u32[]{:S(2)}, u32[]{:S(2)}) collective-permute-start(bf16[2,4,2304]{2,1,0:T(4,128)(2,1)S(1)} %precondition_neighbour.1), channel_id=1, source_target_pairs={{0,3},{1,2},{2,5},{3,4},{4,7},{5,6},{6,1},{7,0},{8,11},{9,10},{10,... | collective-permute-start | bytes 110600 | tf_op jit(solution)/shard_map/ppermute | solution.py:174
  7.0 4.3 %collective-permute-start.4 = (bf16[2,4,2304]{2,1,0:T(4,128)(2,1)S(1)}, bf16[2,4,2304]{2,1,0:T(4,128)(2,1)S(1)}, u32[]{:S(2)}, u32[]{:S(2)}) collective-permute-start(bf16[2,4,2304]{2,1,0:T(4,128)(2,1)S(1)} %precondition_neighbour.1), channel_id=1, source_target_pairs={{0,4},{2,6},{4,0},{6,2},{8,12},{10,14},{12,8},{14,10},{1,5},{3,7},... | collective-permute-start | bytes 110600 | tf_op jit(solution)/shard_map/ppermute | solution.py:174
  8.7 4.1 %collective-permute-start.3 = (bf16[2,4,2304]{2,1,0:T(4,128)(2,1)S(1)}, bf16[2,4,2304]{2,1,0:T(4,128)(2,1)S(1)}, u32[]{:S(2)}, u32[]{:S(2)}) collective-permute-start(bf16[2,4,2304]{2,1,0:T(4,128)(2,1)S(1)} %precondition_neighbour.1), channel_id=1, source_target_pairs={{0,6},{2,0},{4,2},{6,4},{8,14},{10,8},{12,10},{14,12},{1,7},{3,1},... | collective-permute-start | bytes 110600 | tf_op jit(solution)/shard_map/ppermute | solution.py:174
  11.0 1.8 %collective-permute-start.2 = (bf16[2,4,2304]{2,1,0:T(4,128)(2,1)S(1)}, bf16[2,4,2304]{2,1,0:T(4,128)(2,1)S(1)}, u32[]{:S(2)}, u32[]{:S(2)}) collective-permute-start(bf16[2,4,2304]{2,1,0:T(4,128)(2,1)S(1)} %collective-permute-done.1), channel_id=1, source_target_pairs={{0,1},{1,0},{2,3},{3,2},{4,5},{5,4},{6,7},{7,6},{8,9},{9,8},{10,11... | collective-permute-start | bytes 110600 | tf_op jit(solution)/shard_map/ppermute | solution.py:174
  13.6 1.2 %collective-permute-start.5 = (f32[4,128]{1,0:T(4,128)S(1)}, f32[4,128]{1,0:T(4,128)S(1)}, u32[]{:S(2)}, u32[]{:S(2)}) collective-permute-start(f32[4,128]{1,0:T(4,128)S(1)} %select_select_fusion), channel_id=1, source_target_pairs={{0,1},{1,0},{2,3},{3,2},{4,5},{5,4},{6,7},{7,6},{8,9},{9,8},{10,11... | collective-permute-start | bytes 6152 | tf_op jit(solution)/shard_map/ppermute | solution.py:206
